TPU v7x, 128 devices: a whole 4x4x4 slice. The times are simulated.
128 devices in a mesh: shot: 4 (over x_hi, core), gx: 4 (over z), gy: 8 (over x_lo, y).
Axes of the slice: x: 4 (x_hi: 2, x_lo: 2; x = x_hi * 2 + x_lo), y: 4, z: 4, core: 2. Of those that a mesh axis runs over, the one named last changes fastest.
Arguments:
- velocity: bfloat16 [512, 256, 256], P(('shot', 'gx'), 'gy'), may hold values from 0.14941406 to 0.34960938
- epsilon: bfloat16 [512, 256, 256], P(('shot', 'gx'), 'gy'), may hold values from 0.049804688 to 0.29882812
- delta: bfloat16 [512, 256, 256], P(('shot', 'gx'), 'gy'), may hold values from 0.019897461 to 0.14941406
- anchors: int32 [4], replicated, may hold values from 0 to 384
- sources: int32 [4, 3], P('shot'), may hold values from 0 to 255, as said below
- wavelet: float32 [4, 4], P('shot'), may hold values from -8 to 8
- p_now: float32 [4, 128, 256, 256], P('shot', 'gx', 'gy'), may hold values from -6 to 6
- p_prev: float32 [4, 128, 256, 256], P('shot', 'gx', 'gy'), may hold values from -6 to 6
- q_now: float32 [4, 128, 256, 256], P('shot', 'gx', 'gy'), may hold values from -6 to 6
- q_prev: float32 [4, 128, 256, 256], P('shot', 'gx', 'gy'), may hold values from -6 to 6
Outputs:
- p_out: float32 [4, 128, 256, 256], P('shot', 'gx', 'gy')
- q_out: float32 [4, 128, 256, 256], P('shot', 'gx', 'gy')
Inputs may be any that keep to these rules, and one draw needn't show every extreme that they name: `sources`: each source lies inside its aperture: x below 128, y below 256, z below 256; some source lies on the aperture's far end along its longest dimension, and some source has x equal to 0.
All inputs are finite; a program needn't handle non-finite values.
Results may differ from a plain program's by a relative error of at most 0.0003.
Values may be sent and summed in bfloat16 or wider, within the bound.
A program may use at most 128 MiB of HBM per device.

v0:
```python
import jax
import jax.numpy as jnp
from jax import lax
from jax.sharding import PartitionSpec as P

STEPS = 4
STENCIL_WEIGHTS = (-205.0 / 72.0, 8.0 / 5.0, -1.0 / 5.0, 8.0 / 315.0, -1.0 / 560.0)


def with_halo(block, sides, width):
    for axis, dim in sides:
        count = lax.axis_size(axis)
        forward = [(i, i + 1) for i in range(count - 1)]
        backward = [(target, source) for source, target in forward]
        low = lax.ppermute(
            lax.slice_in_dim(block, block.shape[dim] - width, None, axis=dim), axis, forward
        )
        high = lax.ppermute(lax.slice_in_dim(block, 0, width, axis=dim), axis, backward)
        block = jnp.concatenate([low, block, high], axis=dim)
    return block


def shifted_up(values, reach):
    filler = jnp.zeros(values.shape[:-1] + (reach,), values.dtype)
    return jnp.concatenate([values[..., reach:], filler], -1)


def shifted_down(values, reach):
    filler = jnp.zeros(values.shape[:-1] + (reach,), values.dtype)
    return jnp.concatenate([filler, values[..., :-reach]], -1)


def vertical_second(values):
    total = STENCIL_WEIGHTS[0] * values
    for reach in range(1, 5):
        total = total + STENCIL_WEIGHTS[reach] * (
            shifted_up(values, reach) + shifted_down(values, reach)
        )
    return total


def horizontal_second(padded, x_count, y_count):
    x_total = STENCIL_WEIGHTS[0] * padded[4 : 4 + x_count, 4 : 4 + y_count]
    for reach in range(1, 5):
        x_total = x_total + STENCIL_WEIGHTS[reach] * (
            padded[4 + reach : 4 + reach + x_count, 4 : 4 + y_count]
            + padded[4 - reach : 4 - reach + x_count, 4 : 4 + y_count]
        )
    y_total = STENCIL_WEIGHTS[0] * padded[4 : 4 + x_count, 4 : 4 + y_count]
    for reach in range(1, 5):
        y_total = y_total + STENCIL_WEIGHTS[reach] * (
            padded[4 : 4 + x_count, 4 + reach : 4 + reach + y_count]
            + padded[4 : 4 + x_count, 4 - reach : 4 - reach + y_count]
        )
    return x_total + y_total


def update(padded_p, p_field, p_before, q_field, q_before, courant_sq, horiz_gain, cross_gain):
    laplace_h = horizontal_second(padded_p, p_field.shape[0], p_field.shape[1])
    depth_term = vertical_second(q_field)
    p_next = (
        2.0 * p_field - p_before + courant_sq * (horiz_gain * laplace_h + cross_gain * depth_term)
    )
    q_next = 2.0 * q_field - q_before + courant_sq * (cross_gain * laplace_h + depth_term)
    return (p_next, q_next)


def window_rows(pieces, offset, row_count):
    total_rows = pieces.shape[0]
    padded = jnp.pad(pieces, ((row_count, row_count), (0, 0), (0, 0)))
    begin_at = jnp.clip(offset + row_count, 0, total_rows + row_count)
    return lax.dynamic_slice_in_dim(padded, begin_at, row_count, 0)


def source_mask(sources, x_count, y_count, z_count, x_first, y_first):
    x_match = (jnp.arange(x_count, dtype=jnp.int32) + x_first == sources[0, 0]).astype(jnp.float32)
    y_match = (jnp.arange(y_count, dtype=jnp.int32) + y_first == sources[0, 1]).astype(jnp.float32)
    z_match = (jnp.arange(z_count, dtype=jnp.int32) == sources[0, 2]).astype(jnp.float32)
    return x_match[:, None, None] * y_match[None, :, None] * z_match[None, None, :]


def on_device(velocity, epsilon, delta, anchors, sources, wavelet, p_now, p_prev, q_now, q_prev):
    x_cells = p_now.shape[1]
    y_cells = p_now.shape[2]
    z_cells = p_now.shape[3]
    shot_index = lax.axis_index("shot")
    x_index = lax.axis_index("gx")
    y_index = lax.axis_index("gy")
    base_row = anchors[shot_index] + x_index * x_cells
    pieces = (
        lax.all_gather(velocity, ("shot", "gx"), axis=0, tiled=True),
        lax.all_gather(epsilon, ("shot", "gx"), axis=0, tiled=True),
        lax.all_gather(delta, ("shot", "gx"), axis=0, tiled=True),
    )
    velocity_block, epsilon_block, delta_block = tuple(
        (window_rows(piece_one, base_row, x_cells) for piece_one in pieces)
    )
    courant_sq = velocity_block.astype(jnp.float32) * velocity_block.astype(jnp.float32)
    horiz_gain = 1.0 + 2.0 * epsilon_block.astype(jnp.float32)
    cross_gain = jnp.sqrt(1.0 + 2.0 * delta_block.astype(jnp.float32))
    x_first = x_index * x_cells
    y_first = y_index * y_cells
    inner_source = source_mask(sources, x_cells, y_cells, z_cells, x_first, y_first)
    p_field = p_now[0]
    p_before = p_prev[0]
    q_field = q_now[0]
    q_before = q_prev[0]
    for step_index in range(STEPS):
        padded = with_halo(p_field, (("gx", 0), ("gy", 1)), 4)
        p_next, q_next = update(
            padded, p_field, p_before, q_field, q_before, courant_sq, horiz_gain, cross_gain
        )
        p_next = p_next + wavelet[0, step_index] * inner_source
        p_before, p_field, q_before, q_field = (p_field, p_next, q_field, q_next)
    return (p_field[None], q_field[None])


def solution(mesh):
    return jax.shard_map(
        on_device,
        mesh=mesh,
        in_specs=(
            P(("shot", "gx"), "gy", None),
            P(("shot", "gx"), "gy", None),
            P(("shot", "gx"), "gy", None),
            P(),
            P("shot", None),
            P("shot", None),
            P("shot", "gx", "gy", None),
            P("shot", "gx", "gy", None),
            P("shot", "gx", "gy", None),
            P("shot", "gx", "gy", None),
        ),
        out_specs=(P("shot", "gx", "gy", None), P("shot", "gx", "gy", None)),
        check_vma=False,
    )
```

profile of v0, /device:TPU:2, one launch (start us, length us, event | category | flops | bytes accessed | tf_op | source)
XLA Modules:
  0.0 381.0 jit_solution(8481441208767258015)
XLA Ops:
  7.2 0.7 all-gather.4.cloned.1.call-update
  8.0 0.7 all-gather.6.cloned.1.call-update
  8.7 0.7 all-gather.8.cloned.1.call-update
  9.4 3.8 %collective-permute-start.1 = (f32[4,32,256]{2,1,0:T(8,128)S(1)}, f32[4,32,256]{2,1,0:T(8,128)S(1)}, u32[]{:S(2)}, u32[]{:S(2)}) collective-permute-start(f32[4,32,256]{2,1,0:T(8,128)S(1)} %get-tuple-element.68), channel_id=1, source_target_pairs={{0,8},{8,16},{16,24},{1,9},{9,17},{17,25},{2,10},{10,18},{18,26},{... | collective-permute-start | bytes 393224 | tf_op jit(solution)/shard_map/ppermute | solution.py:15
  13.3 1.3 collective-permute-start
  14.6 0.6 fusion.139
  15.2 1.3 compare_convert_fusion.1
  16.5 1.7 fusion.135
  18.2 1.7 fusion.136
  19.9 1.7 fusion.134
  21.6 1.7 fusion.137
  23.3 0.1 broadcast_multiply_fusion
  23.4 4.9 %collective-permute-start.2 = (f32[40,4,256]{2,1,0:T(4,128)S(1)}, f32[40,4,256]{2,1,0:T(4,128)S(1)}, u32[]{:S(2)}, u32[]{:S(2)}) collective-permute-start(f32[40,4,256]{2,1,0:T(4,128)S(1)} %get-tuple-element.28), channel_id=1, source_target_pairs={{1,0},{2,1},{3,2},{4,3},{5,4},{6,5},{7,6},{9,8},{10,9},{11,10},{12... | collective-permute-start | bytes 491528 | tf_op jit(solution)/shard_map/ppermute | solution.py:18
  28.4 1.9 collective-permute-start.3
  30.3 0.6 compare_convert_fusion
  30.9 0.6 dynamic_slice.12
  32.0 0.6 fusion.138
  32.7 0.2 collective-permute-done.2
  32.8 4.9 %collective-permute-done.3 = f32[40,4,256]{2,1,0:T(4,128)S(1)} collective-permute-done((f32[40,4,256]{2,1,0:T(4,128)S(1)}, f32[40,4,256]{2,1,0:T(4,128)S(1)}, u32[]{:S(2)}, u32[]{:S(2)}) %collective-permute-start.3) | collective-permute-done | bytes 163872 | tf_op jit(solution)/shard_map/ppermute | solution.py:15
  37.7 2.0 pad_maximum_fusion
  39.7 45.4 %all-gather.4.cloned.1.call-done = bf16[512,32,256]{2,1,0:T(8,128)(2,1)} async-done(((bf16[32,32,256]{2,1,0:T(8,128)(2,1)}), bf16[512,32,256]{2,1,0:T(8,128)(2,1)}) %all-gather.4.cloned.1.call-update) | async-done | bytes 8388624 | tf_op jit(solution)/shard_map/all_gather | solution.py:91
  85.1 73.3 %all-gather.6.cloned.1.call-done = bf16[512,32,256]{2,1,0:T(8,128)(2,1)} async-done(((bf16[32,32,256]{2,1,0:T(8,128)(2,1)}), bf16[512,32,256]{2,1,0:T(8,128)(2,1)}) %all-gather.6.cloned.1.call-update) | async-done | bytes 8388624 | tf_op jit(solution)/shard_map/all_gather | solution.py:92
  158.5 73.3 %all-gather.8.cloned.1.call-done = bf16[512,32,256]{2,1,0:T(8,128)(2,1)} async-done(((bf16[32,32,256]{2,1,0:T(8,128)(2,1)}), bf16[512,32,256]{2,1,0:T(8,128)(2,1)}) %all-gather.8.cloned.1.call-update) | async-done | bytes 8388624 | tf_op jit(solution)/shard_map/all_gather | solution.py:93
  231.8 12.7 %fusion.68 = (f32[32,32,256]{2,1,0:T(8,128)S(1)}, f32[32,32,256]{2,1,0:T(8,128)S(1)}, f32[32,32,256]{2,1,0:T(8,128)}) fusion(f32[1,32,32,256]{3,2,1,0:T(8,128)} %param.17, f32[256]{0:T(256)S(1)} %compare_convert_fusion, f32[32,32]{1,0:T(8,128)S(1)} %broadcast_multiply_fusion, f32[]{:T(128)} %bitcast.6, f32[1,32,32,256]{3,2,1,0:T(8,128)S(1)} %copy-done.1, ...), kind=kLoop, calls=%fused_computation.131 | loop fusion | flops 17039360 | bytes 49468424 | tf_op jit(solution)/shard_map/add | solution.py:113
  244.6 2.8 fusion.113
  247.3 1.7 fusion.131
  249.0 1.7 fusion.130
  250.8 2.1 collective-permute-start.5
  252.9 1.3 collective-permute-start.4
  254.2 1.7 fusion.132
  255.9 4.1 %collective-permute-done.4 = f32[4,32,256]{2,1,0:T(8,128)S(1)} collective-permute-done((f32[4,32,256]{2,1,0:T(8,128)S(1)}, f32[4,32,256]{2,1,0:T(8,128)S(1)}, u32[]{:S(2)}, u32[]{:S(2)}) %collective-permute-start.4) | collective-permute-done | bytes 131104 | tf_op jit(solution)/shard_map/ppermute | solution.py:18
  260.1 5.5 %collective-permute-start.6 = (f32[40,4,256]{2,1,0:T(4,128)S(1)}, f32[40,4,256]{2,1,0:T(4,128)S(1)}, u32[]{:S(2)}, u32[]{:S(2)}) collective-permute-start(f32[40,4,256]{2,1,0:T(4,128)S(1)} %get-tuple-element.24), channel_id=1, source_target_pairs={{1,0},{2,1},{3,2},{4,3},{5,4},{6,5},{7,6},{9,8},{10,9},{11,10},{12... | collective-permute-start | bytes 491528 | tf_op jit(solution)/shard_map/ppermute | solution.py:18
  265.7 2.1 collective-permute-start.7
  267.8 1.7 fusion.129
  269.4 5.5 %collective-permute-done.7 = f32[40,4,256]{2,1,0:T(4,128)S(1)} collective-permute-done((f32[40,4,256]{2,1,0:T(4,128)S(1)}, f32[40,4,256]{2,1,0:T(4,128)S(1)}, u32[]{:S(2)}, u32[]{:S(2)}) %collective-permute-start.7) | collective-permute-done | bytes 163872 | tf_op jit(solution)/shard_map/ppermute | solution.py:15
  275.0 2.0 pad_maximum_fusion.1
  277.0 12.2 %fusion.69 = (f32[32,32,256]{2,1,0:T(8,128)S(1)}, f32[32,32,256]{2,1,0:T(8,128)}, f32[32,32,256]{2,1,0:T(8,128)}) fusion(f32[32,32,256]{2,1,0:T(8,128)S(1)} %get-tuple-element.11, f32[]{:T(128)} %bitcast.11, f32[256]{0:T(256)S(1)} %compare_convert_fusion, f32[32,32]{1,0:T(8,128)S(1)} %broadcast_multiply_fusion, f32[1,32,32,256]{3,2,1,0:T(8,128)S(1)} %copy-done.1, ...), kind=kLoop, calls=%fused_computation.132 | loop fusion | flops 17039360 | bytes 48419848 | tf_op jit(solution)/shard_map/add | solution.py:113
  289.2 2.4 multiply_add_fusion.3
  291.6 1.7 fusion.126
  293.3 1.7 fusion.125
  295.0 3.1 collective-permute-start.9
  298.2 1.3 collective-permute-start.8
  299.5 1.7 fusion.127
  301.2 3.9 %collective-permute-done.8 = f32[4,32,256]{2,1,0:T(8,128)S(1)} collective-permute-done((f32[4,32,256]{2,1,0:T(8,128)S(1)}, f32[4,32,256]{2,1,0:T(8,128)S(1)}, u32[]{:S(2)}, u32[]{:S(2)}) %collective-permute-start.8) | collective-permute-done | bytes 131104 | tf_op jit(solution)/shard_map/ppermute | solution.py:18
  305.1 1.9 collective-permute-start.10
  307.0 3.9 %collective-permute-start.11 = (f32[40,4,256]{2,1,0:T(4,128)S(1)}, f32[40,4,256]{2,1,0:T(4,128)S(1)}, u32[]{:S(2)}, u32[]{:S(2)}) collective-permute-start(f32[40,4,256]{2,1,0:T(4,128)S(1)} %get-tuple-element.21), channel_id=1, source_target_pairs={{0,1},{1,2},{2,3},{3,4},{4,5},{5,6},{6,7},{8,9},{9,10},{10,11},{11... | collective-permute-start | bytes 491528 | tf_op jit(solution)/shard_map/ppermute | solution.py:15
  311.0 1.7 fusion.124
  312.6 3.7 collective-permute-done.11
  316.4 2.0 pad_maximum_fusion.2
  318.3 12.2 %fusion.70 = (f32[32,32,256]{2,1,0:T(8,128)S(1)}, f32[32,32,256]{2,1,0:T(8,128)}, f32[32,32,256]{2,1,0:T(8,128)}) fusion(f32[32,32,256]{2,1,0:T(8,128)S(1)} %copy-done.3, f32[32,32,256]{2,1,0:T(8,128)S(1)} %get-tuple-element.8, f32[]{:T(128)} %bitcast.12, f32[256]{0:T(256)S(1)} %compare_convert_fusion, f32[32,32]{1,0:T(8,128)S(1)} %broadcast_multiply_fusion, ...), kind=kLoop, calls=%fused_computation.133 | loop fusion | flops 17039360 | bytes 48419848 | tf_op jit(solution)/shard_map/add | solution.py:113
  330.5 2.4 multiply_add_fusion.1
  333.0 1.7 fusion.122
  334.7 1.8 fusion.120
  336.4 2.9 collective-permute-start.13
  339.4 1.3 collective-permute-start.12
  340.7 1.7 fusion.121
  342.4 3.8 %collective-permute-done.12 = f32[4,32,256]{2,1,0:T(8,128)S(1)} collective-permute-done((f32[4,32,256]{2,1,0:T(8,128)S(1)}, f32[4,32,256]{2,1,0:T(8,128)S(1)}, u32[]{:S(2)}, u32[]{:S(2)}) %collective-permute-start.12) | collective-permute-done | bytes 131104 | tf_op jit(solution)/shard_map/ppermute | solution.py:18
  346.3 1.9 collective-permute-start.14
  348.2 4.1 %collective-permute-start.15 = (f32[40,4,256]{2,1,0:T(4,128)S(1)}, f32[40,4,256]{2,1,0:T(4,128)S(1)}, u32[]{:S(2)}, u32[]{:S(2)}) collective-permute-start(f32[40,4,256]{2,1,0:T(4,128)S(1)} %get-tuple-element.17), channel_id=1, source_target_pairs={{0,1},{1,2},{2,3},{3,4},{4,5},{5,6},{6,7},{8,9},{9,10},{10,11},{11... | collective-permute-start | bytes 491528 | tf_op jit(solution)/shard_map/ppermute | solution.py:15
  352.4 1.7 fusion.119
  354.1 3.5 collective-permute-done.15
  357.6 2.0 pad_maximum_fusion.3
  359.5 10.9 %add_bitcast_fusion = (f32[1,32,32,256]{3,2,1,0:T(8,128)}, f32[32,32,256]{2,1,0:T(8,128)S(1)}, f32[32,32,256]{2,1,0:T(8,128)}) fusion(f32[32,32,256]{2,1,0:T(8,128)S(1)} %multiply_add_fusion.3, f32[32,32,256]{2,1,0:T(8,128)S(1)} %multiply_add_fusion.1, s32[]{:T(128)S(6)} %min.6, bf16[512,32,256]{2,1,0:T(8,128)(2,1)S(1)} %bitcast.35, ...), kind=kLoop, calls=%fused_computation.204 | loop fusion | flops 15204352 | bytes 40026116 | tf_op jit(solution)/shard_map/broadcast_in_dim | solution.py:115
  370.5 4.0 %fusion.72 = f32[1,32,32,256]{3,2,1,0:T(8,128)} fusion(f32[32,32,256]{2,1,0:T(8,128)} %get-tuple-element.4, f32[32,32,256]{2,1,0:T(8,128)S(1)} %get-tuple-element.3, f32[32,32,256]{2,1,0:T(8,128)S(1)} %get-tuple-element.8, f32[32,32,256]{2,1,0:T(8,128)S(1)} %get-tuple-element.5, f32[]{:T(128)} %bitcast.13, f32[256]{0:T(256)S(1)} %compare_convert_fusion, ...), kind=kLoop, calls=%fused_computation.135 | loop fusion | flops 4718592 | bytes 30413832 | tf_op jit(solution)/shard_map/broadcast_in_dim | solution.py:115
  (38 shorter events, 0.5 us)
Async XLA Ops:
  7.2 2.3 copy-start.1
  7.2 7.4 %copy-start.5 = (s32[1,3]{1,0:T(1,128)S(1)}, s32[1,3]{1,0:T(1,128)}, u32[]{:S(2)}) copy-start(s32[1,3]{1,0:T(1,128)} %param.14) | copy-start | bytes 40
  7.2 9.3 %copy-start = (f32[1,32,32,256]{3,2,1,0:T(8,128)S(1)}, f32[1,32,32,256]{3,2,1,0:T(8,128)}, u32[]{:S(2)}) copy-start(f32[1,32,32,256]{3,2,1,0:T(8,128)} %param.18) | copy-start | bytes 3145732
  7.2 77.9 %all-gather.4.cloned.1.call-start = ((), (), s32[]{:S(2)}) async-start(), calls=%async_computation | async-start | bytes 8912896 | tf_op jit(solution)/shard_map/all_gather | solution.py:91
  7.9 150.5 %all-gather.6.cloned.1.call-start = ((), (), s32[]{:S(2)}) async-start(), calls=%async_computation.1 | async-start | bytes 8912896 | tf_op jit(solution)/shard_map/all_gather | solution.py:92
  8.7 223.1 %all-gather.8.cloned.1.call-start = ((), (), s32[]{:S(2)}) async-start(), calls=%async_computation.2 | async-start | bytes 8912896 | tf_op jit(solution)/shard_map/all_gather | solution.py:93
  9.4 13.9 %collective-permute-start.1 = (f32[4,32,256]{2,1,0:T(8,128)S(1)}, f32[4,32,256]{2,1,0:T(8,128)S(1)}, u32[]{:S(2)}, u32[]{:S(2)}) collective-permute-start(f32[4,32,256]{2,1,0:T(8,128)S(1)} %get-tuple-element.68), channel_id=1, source_target_pairs={{0,8},{8,16},{16,24},{1,9},{9,17},{17,25},{2,10},{10,18},{18,26},{... | collective-permute-start | bytes 393224 | tf_op jit(solution)/shard_map/ppermute | solution.py:15
  13.3 10.1 %collective-permute-start = (f32[4,32,256]{2,1,0:T(8,128)S(1)}, f32[4,32,256]{2,1,0:T(8,128)S(1)}, u32[]{:S(2)}, u32[]{:S(2)}) collective-permute-start(f32[4,32,256]{2,1,0:T(8,128)S(1)} %get-tuple-element.69), channel_id=1, source_target_pairs={{8,0},{16,8},{24,16},{9,1},{17,9},{25,17},{10,2},{18,10},{26,18},{... | collective-permute-start | bytes 393224 | tf_op jit(solution)/shard_map/ppermute | solution.py:18
  23.3 7.6 %copy-start.6 = (s32[4]{0:T(128)S(1)}, s32[4]{0:T(128)}, u32[]{:S(2)}) copy-start(s32[4]{0:T(128)} %param.13) | copy-start | bytes 52
  23.3 8.7 %copy-start.4 = (f32[1,4]{1,0:T(1,128)S(1)}, f32[1,4]{1,0:T(1,128)}, u32[]{:S(2)}) copy-start(f32[1,4]{1,0:T(1,128)} %param.15) | copy-start | bytes 52
  23.4 9.4 %collective-permute-start.2 = (f32[40,4,256]{2,1,0:T(4,128)S(1)}, f32[40,4,256]{2,1,0:T(4,128)S(1)}, u32[]{:S(2)}, u32[]{:S(2)}) collective-permute-start(f32[40,4,256]{2,1,0:T(4,128)S(1)} %get-tuple-element.28), channel_id=1, source_target_pairs={{1,0},{2,1},{3,2},{4,3},{5,4},{6,5},{7,6},{9,8},{10,9},{11,10},{12... | collective-permute-start | bytes 491528 | tf_op jit(solution)/shard_map/ppermute | solution.py:18
  28.4 9.4 %collective-permute-start.3 = (f32[40,4,256]{2,1,0:T(4,128)S(1)}, f32[40,4,256]{2,1,0:T(4,128)S(1)}, u32[]{:S(2)}, u32[]{:S(2)}) collective-permute-start(f32[40,4,256]{2,1,0:T(4,128)S(1)} %get-tuple-element.29), channel_id=1, source_target_pairs={{0,1},{1,2},{2,3},{3,4},{4,5},{5,6},{6,7},{8,9},{9,10},{10,11},{11... | collective-permute-start | bytes 491528 | tf_op jit(solution)/shard_map/ppermute | solution.py:15
  231.8 12.7 %slice-start = ((s8[8388608]{0:T(1024)(128)(4,1)}), s8[4194304]{0:T(1024)(128)(4,1)S(1)}, s32[]{:S(2)}) async-start(s8[8388608]{0:T(1024)(128)(4,1)} %bitcast.34), calls=%async_computation.3 | async-start | bytes 8388608
  231.8 12.7 %slice-start.1 = ((s8[8388608]{0:T(1024)(128)(4,1)}), s8[4194304]{0:T(1024)(128)(4,1)S(1)}, s32[]{:S(2)}) async-start(s8[8388608]{0:T(1024)(128)(4,1)} %bitcast.34), calls=%async_computation.4 | async-start | bytes 8388608
  244.5 32.4 %copy-start.2 = (f32[32,32,256]{2,1,0:T(8,128)}, f32[32,32,256]{2,1,0:T(8,128)S(1)}, u32[]{:S(2)}) copy-start(f32[32,32,256]{2,1,0:T(8,128)S(1)} %get-tuple-element.11) | copy-start | bytes 3145732
  250.8 5.1 %collective-permute-start.5 = (f32[4,32,256]{2,1,0:T(8,128)S(1)}, f32[4,32,256]{2,1,0:T(8,128)S(1)}, u32[]{:S(2)}, u32[]{:S(2)}) collective-permute-start(f32[4,32,256]{2,1,0:T(8,128)S(1)} %get-tuple-element.58), channel_id=1, source_target_pairs={{0,8},{8,16},{16,24},{1,9},{9,17},{17,25},{2,10},{10,18},{18,26},{... | collective-permute-start | bytes 393224 | tf_op jit(solution)/shard_map/ppermute | solution.py:15
  252.9 7.2 %collective-permute-start.4 = (f32[4,32,256]{2,1,0:T(8,128)S(1)}, f32[4,32,256]{2,1,0:T(8,128)S(1)}, u32[]{:S(2)}, u32[]{:S(2)}) collective-permute-start(f32[4,32,256]{2,1,0:T(8,128)S(1)} %get-tuple-element.59), channel_id=1, source_target_pairs={{8,0},{16,8},{24,16},{9,1},{17,9},{25,17},{10,2},{18,10},{26,18},{... | collective-permute-start | bytes 393224 | tf_op jit(solution)/shard_map/ppermute | solution.py:18
  260.1 9.3 %collective-permute-start.6 = (f32[40,4,256]{2,1,0:T(4,128)S(1)}, f32[40,4,256]{2,1,0:T(4,128)S(1)}, u32[]{:S(2)}, u32[]{:S(2)}) collective-permute-start(f32[40,4,256]{2,1,0:T(4,128)S(1)} %get-tuple-element.24), channel_id=1, source_target_pairs={{1,0},{2,1},{3,2},{4,3},{5,4},{6,5},{7,6},{9,8},{10,9},{11,10},{12... | collective-permute-start | bytes 491528 | tf_op jit(solution)/shard_map/ppermute | solution.py:18
  265.7 9.3 %collective-permute-start.7 = (f32[40,4,256]{2,1,0:T(4,128)S(1)}, f32[40,4,256]{2,1,0:T(4,128)S(1)}, u32[]{:S(2)}, u32[]{:S(2)}) collective-permute-start(f32[40,4,256]{2,1,0:T(4,128)S(1)} %get-tuple-element.25), channel_id=1, source_target_pairs={{0,1},{1,2},{2,3},{3,4},{4,5},{5,6},{6,7},{8,9},{9,10},{10,11},{11... | collective-permute-start | bytes 491528 | tf_op jit(solution)/shard_map/ppermute | solution.py:15
  295.0 6.1 %collective-permute-start.9 = (f32[4,32,256]{2,1,0:T(8,128)S(1)}, f32[4,32,256]{2,1,0:T(8,128)S(1)}, u32[]{:S(2)}, u32[]{:S(2)}) collective-permute-start(f32[4,32,256]{2,1,0:T(8,128)S(1)} %get-tuple-element.48), channel_id=1, source_target_pairs={{0,8},{8,16},{16,24},{1,9},{9,17},{17,25},{2,10},{10,18},{18,26},{... | collective-permute-start | bytes 393224 | tf_op jit(solution)/shard_map/ppermute | solution.py:15
  298.2 6.9 %collective-permute-start.8 = (f32[4,32,256]{2,1,0:T(8,128)S(1)}, f32[4,32,256]{2,1,0:T(8,128)S(1)}, u32[]{:S(2)}, u32[]{:S(2)}) collective-permute-start(f32[4,32,256]{2,1,0:T(8,128)S(1)} %get-tuple-element.49), channel_id=1, source_target_pairs={{8,0},{16,8},{24,16},{9,1},{17,9},{25,17},{10,2},{18,10},{26,18},{... | collective-permute-start | bytes 393224 | tf_op jit(solution)/shard_map/ppermute | solution.py:18
  305.1 7.5 %collective-permute-start.10 = (f32[40,4,256]{2,1,0:T(4,128)S(1)}, f32[40,4,256]{2,1,0:T(4,128)S(1)}, u32[]{:S(2)}, u32[]{:S(2)}) collective-permute-start(f32[40,4,256]{2,1,0:T(4,128)S(1)} %get-tuple-element.20), channel_id=1, source_target_pairs={{1,0},{2,1},{3,2},{4,3},{5,4},{6,5},{7,6},{9,8},{10,9},{11,10},{12... | collective-permute-start | bytes 491528 | tf_op jit(solution)/shard_map/ppermute | solution.py:18
  307.0 9.3 %collective-permute-start.11 = (f32[40,4,256]{2,1,0:T(4,128)S(1)}, f32[40,4,256]{2,1,0:T(4,128)S(1)}, u32[]{:S(2)}, u32[]{:S(2)}) collective-permute-start(f32[40,4,256]{2,1,0:T(4,128)S(1)} %get-tuple-element.21), channel_id=1, source_target_pairs={{0,1},{1,2},{2,3},{3,4},{4,5},{5,6},{6,7},{8,9},{9,10},{10,11},{11... | collective-permute-start | bytes 491528 | tf_op jit(solution)/shard_map/ppermute | solution.py:15
  312.6 5.7 %copy-start.3 = (f32[32,32,256]{2,1,0:T(8,128)S(1)}, f32[32,32,256]{2,1,0:T(8,128)}, u32[]{:S(2)}) copy-start(f32[32,32,256]{2,1,0:T(8,128)} %copy-done.2) | copy-start | bytes 3145732
  336.4 6.0 %collective-permute-start.13 = (f32[4,32,256]{2,1,0:T(8,128)S(1)}, f32[4,32,256]{2,1,0:T(8,128)S(1)}, u32[]{:S(2)}, u32[]{:S(2)}) collective-permute-start(f32[4,32,256]{2,1,0:T(8,128)S(1)} %get-tuple-element.38), channel_id=1, source_target_pairs={{0,8},{8,16},{16,24},{1,9},{9,17},{17,25},{2,10},{10,18},{18,26},{... | collective-permute-start | bytes 393224 | tf_op jit(solution)/shard_map/ppermute | solution.py:15
  339.4 6.9 %collective-permute-start.12 = (f32[4,32,256]{2,1,0:T(8,128)S(1)}, f32[4,32,256]{2,1,0:T(8,128)S(1)}, u32[]{:S(2)}, u32[]{:S(2)}) collective-permute-start(f32[4,32,256]{2,1,0:T(8,128)S(1)} %get-tuple-element.39), channel_id=1, source_target_pairs={{8,0},{16,8},{24,16},{9,1},{17,9},{25,17},{10,2},{18,10},{26,18},{... | collective-permute-start | bytes 393224 | tf_op jit(solution)/shard_map/ppermute | solution.py:18
  346.3 7.8 %collective-permute-start.14 = (f32[40,4,256]{2,1,0:T(4,128)S(1)}, f32[40,4,256]{2,1,0:T(4,128)S(1)}, u32[]{:S(2)}, u32[]{:S(2)}) collective-permute-start(f32[40,4,256]{2,1,0:T(4,128)S(1)} %get-tuple-element.16), channel_id=1, source_target_pairs={{1,0},{2,1},{3,2},{4,3},{5,4},{6,5},{7,6},{9,8},{10,9},{11,10},{12... | collective-permute-start | bytes 491528 | tf_op jit(solution)/shard_map/ppermute | solution.py:18
  348.2 9.3 %collective-permute-start.15 = (f32[40,4,256]{2,1,0:T(4,128)S(1)}, f32[40,4,256]{2,1,0:T(4,128)S(1)}, u32[]{:S(2)}, u32[]{:S(2)}) collective-permute-start(f32[40,4,256]{2,1,0:T(4,128)S(1)} %get-tuple-element.17), channel_id=1, source_target_pairs={{0,1},{1,2},{2,3},{3,4},{4,5},{5,6},{6,7},{8,9},{9,10},{10,11},{11... | collective-permute-start | bytes 491528 | tf_op jit(solution)/shard_map/ppermute | solution.py:15
Sparse Core Ops, SparseCore 0:
  10.5 74.5 all-gather.3
  87.6 70.8 all-gather.5
  160.9 70.8 all-gather.7
where the time goes:
time: 382 us; the launch traced here: 381 us
  waiting for transfers between devices  224 us (59%)
  other arithmetic  69.8 us (18%)
  starting transfers between devices  43.6 us (11%)
  local copies, waits for them, and re-layouts  29.1 us (8%)
  between operations  14.7 us (4%)
    all_gather x1, waiting for transfers between devices, on_device(): lax.all_gather(delta, ('shot', 'gx'), axis=0, tiled=True)  73.3 us
    all_gather x1, waiting for transfers between devices, on_device(): lax.all_gather(epsilon, ('shot', 'gx'), axis=0, tiled=True)  73.3 us
    all_gather x1, waiting for transfers between devices, on_device(): lax.all_gather(velocity, ('shot', 'gx'), axis=0, tiled=True)  45.4 us
    add x3, other arithmetic, on_device(): p_next = p_next + wavelet[0, step_index] * inner_source  37.1 us
    slice x16, local copies, waits for them, and re-layouts, shifted_up(): return jnp.concatenate([values[..., reach:], filler], -1)  27.2 us
    ppermute x8, starting transfers between devices, with_halo(): lax.ppermute(lax.slice_in_dim(block, block.shape[dim] - width, None, axis...  24.1 us
    ppermute x8, starting transfers between devices, with_halo(): lax.ppermute(lax.slice_in_dim(block, 0, width, axis=dim), axis, backward)  19.5 us
    ppermute x8, waiting for transfers between devices, with_halo(): lax.ppermute(lax.slice_in_dim(block, block.shape[dim] - width, None, axis...  17.7 us
  transfers between devices with their start and end apart: 19, of which 12 were waited for; matrix products, arithmetic and copies ran while one was open for 6% of the time, Pallas kernels for 0%

commit v1 on v0

--- a/solution.py
+++ b/solution.py
@@ -89,7 +89,12 @@
     base_row = anchors[shot_index] + x_index * x_cells
     pieces = (
         lax.all_gather(velocity, ("shot", "gx"), axis=0, tiled=True),
-        lax.all_gather(epsilon, ("shot", "gx"), axis=0, tiled=True),
+        jnp.concatenate(
+            lax.all_to_all(
+                jnp.stack([epsilon] * lax.axis_size(("shot", "gx"))), ("shot", "gx"), 0, 0
+            ),
+            axis=0,
+        ),
         lax.all_gather(delta, ("shot", "gx"), axis=0, tiled=True),
     )
     velocity_block, epsilon_block, delta_block = tuple(

time: 382 us -> 378 us (0.990)
  waiting for transfers between devices: 224 us -> 199 us
  starting transfers between devices: 43.6 us -> 58.8 us
  local copies, waits for them, and re-layouts: 29.1 us -> 34.4 us
    ppermute x8, waiting for transfers between devices: 12 us -> 99.5 us  [with_halo(): lax.ppermute(lax.slice_in_dim(block, 0, width, axis=dim), axis, backward)]
    all_gather x1 -> x0, waiting for transfers between devices: 73.3 us -> none  [on_device(): lax.all_gather(epsilon, ('shot', 'gx'), axis=0, tiled=True)]
    all_gather x1, waiting for transfers between devices: 45.4 us -> 5.47 us  [on_device(): lax.all_gather(velocity, ('shot', 'gx'), axis=0, tiled=True)]
    all_to_all x0 -> x1, starting transfers between devices: none -> 7.16 us  [on_device(): lax.all_to_all(jnp.stack([epsilon] * lax.axis_size(('shot', 'gx'))), ('sh...]
    ppermute x8, starting transfers between devices: 24.1 us -> 31.1 us  [with_halo(): lax.ppermute(lax.slice_in_dim(block, block.shape[dim] - width, None, axis...]
    another operation x0 -> x1, local copies, waits for them, and re-layouts: none -> 5.37 us  [on_device(): jnp.stack([epsilon] * lax.axis_size(('shot', 'gx')))]
  transfers between devices with their start and end apart: 19 -> 19, of which waited for: 12 -> 10; matrix products, arithmetic and copies ran while one was open for 6% -> 8% of each run, Pallas kernels for 0% -> 0%
where the time goes in v1:
time: 378 us; the launch traced here: 377 us
  waiting for transfers between devices  199 us (53%)
  other arithmetic  69.1 us (18%)
  starting transfers between devices  58.8 us (16%)
  local copies, waits for them, and re-layouts  34.4 us (9%)
  between operations  14.9 us (4%)
    ppermute x8, waiting for transfers between devices, with_halo(): lax.ppermute(lax.slice_in_dim(block, 0, width, axis=dim), axis, backward)  99.5 us
    all_gather x1, waiting for transfers between devices, on_device(): lax.all_gather(delta, ('shot', 'gx'), axis=0, tiled=True)  72.4 us
    add x3, other arithmetic, on_device(): p_next = p_next + wavelet[0, step_index] * inner_source  36.5 us
    ppermute x8, starting transfers between devices, with_halo(): lax.ppermute(lax.slice_in_dim(block, block.shape[dim] - width, None, axis...  31.1 us
    slice x16, local copies, waits for them, and re-layouts, shifted_up(): return jnp.concatenate([values[..., reach:], filler], -1)  27.1 us
    ppermute x8, waiting for transfers between devices, with_halo(): lax.ppermute(lax.slice_in_dim(block, block.shape[dim] - width, None, axis...  20.5 us
    ppermute x8, starting transfers between devices, with_halo(): lax.ppermute(lax.slice_in_dim(block, 0, width, axis=dim), axis, backward)  20.4 us
    broadcast_in_dim x2, other arithmetic, on_device(): return (p_field[None], q_field[None])  14.8 us
  transfers between devices with their start and end apart: 19, of which 10 were waited for; matrix products, arithmetic and copies ran while one was open for 8% of the time, Pallas kernels for 0%

profile of v1, /device:TPU:2, one launch (start us, length us, event | category | flops | bytes accessed | tf_op | source)
XLA Modules:
  0.0 376.6 jit_solution(1482601684562696576)
XLA Ops:
  7.2 0.7 all-gather.3.cloned.1.call-update
  7.9 0.7 all-gather.5.cloned.1.call-update
  8.6 5.4 %stack.2 = bf16[16,32,32,256]{3,2,1,0:T(8,128)(2,1)} broadcast(bf16[32,32,256]{2,1,0:T(8,128)(2,1)} %param.11), dimensions={1,2,3} | broadcast | bytes 8912896 | tf_op jit(solution)/shard_map/stack | solution.py:94
  14.0 7.2 %all-to-all-start = ((bf16[16,32,32,256]{3,2,1,0:T(8,128)(2,1)}), bf16[16,32,32,256]{3,2,1,0:T(8,128)(2,1)}, u32[]{:S(2)}, u32[]{:S(2)}) async-start(bf16[16,32,32,256]{3,2,1,0:T(8,128)(2,1)} %stack.2), calls=%async_computation | async-start | bytes 16777216 | tf_op jit(solution)/shard_map/all_to_all | solution.py:93
  21.2 1.3 collective-permute-start
  22.5 4.6 %collective-permute-start.1 = (f32[4,32,256]{2,1,0:T(8,128)S(1)}, f32[4,32,256]{2,1,0:T(8,128)S(1)}, u32[]{:S(2)}, u32[]{:S(2)}) collective-permute-start(f32[4,32,256]{2,1,0:T(8,128)S(1)} %get-tuple-element.68), channel_id=1, source_target_pairs={{0,8},{8,16},{16,24},{1,9},{9,17},{17,25},{2,10},{10,18},{18,26},{... | collective-permute-start | bytes 393224 | tf_op jit(solution)/shard_map/ppermute | solution.py:15
  27.1 0.6 fusion.139
  27.7 1.3 compare_convert_fusion.1
  29.0 1.7 fusion.137
  30.7 1.7 fusion.136
  32.4 1.7 fusion.135
  34.1 1.7 fusion.134
  35.8 0.1 broadcast_multiply_fusion
  35.9 99.5 %collective-permute-done = f32[4,32,256]{2,1,0:T(8,128)S(1)} collective-permute-done((f32[4,32,256]{2,1,0:T(8,128)S(1)}, f32[4,32,256]{2,1,0:T(8,128)S(1)}, u32[]{:S(2)}, u32[]{:S(2)}) %collective-permute-start) | collective-permute-done | bytes 131104 | tf_op jit(solution)/shard_map/ppermute | solution.py:18
  135.4 5.9 %collective-permute-start.2 = (f32[40,4,256]{2,1,0:T(4,128)S(1)}, f32[40,4,256]{2,1,0:T(4,128)S(1)}, u32[]{:S(2)}, u32[]{:S(2)}) collective-permute-start(f32[40,4,256]{2,1,0:T(4,128)S(1)} %get-tuple-element.28), channel_id=1, source_target_pairs={{1,0},{2,1},{3,2},{4,3},{5,4},{6,5},{7,6},{9,8},{10,9},{11,10},{12... | collective-permute-start | bytes 491528 | tf_op jit(solution)/shard_map/ppermute | solution.py:18
  141.3 1.9 collective-permute-start.3
  143.2 0.6 compare_convert_fusion
  143.8 0.6 dynamic_slice.12
  145.0 0.7 fusion.138
  145.7 5.2 %collective-permute-done.3 = f32[40,4,256]{2,1,0:T(4,128)S(1)} collective-permute-done((f32[40,4,256]{2,1,0:T(4,128)S(1)}, f32[40,4,256]{2,1,0:T(4,128)S(1)}, u32[]{:S(2)}, u32[]{:S(2)}) %collective-permute-start.3) | collective-permute-done | bytes 163872 | tf_op jit(solution)/shard_map/ppermute | solution.py:15
  150.9 2.1 pad_maximum_fusion
  153.0 5.5 %all-gather.3.cloned.1.call-done = bf16[512,32,256]{2,1,0:T(8,128)(2,1)} async-done(((bf16[32,32,256]{2,1,0:T(8,128)(2,1)}), bf16[512,32,256]{2,1,0:T(8,128)(2,1)}) %all-gather.3.cloned.1.call-update) | async-done | bytes 8388624 | tf_op jit(solution)/shard_map/all_gather | solution.py:91
  158.5 72.4 %all-gather.5.cloned.1.call-done = bf16[512,32,256]{2,1,0:T(8,128)(2,1)} async-done(((bf16[32,32,256]{2,1,0:T(8,128)(2,1)}), bf16[512,32,256]{2,1,0:T(8,128)(2,1)}) %all-gather.5.cloned.1.call-update) | async-done | bytes 8388624 | tf_op jit(solution)/shard_map/all_gather | solution.py:98
  230.9 12.5 %fusion.68 = (f32[32,32,256]{2,1,0:T(8,128)S(1)}, f32[32,32,256]{2,1,0:T(8,128)S(1)}, f32[32,32,256]{2,1,0:T(8,128)}) fusion(f32[1,32,32,256]{3,2,1,0:T(8,128)} %param.17, f32[256]{0:T(256)S(1)} %compare_convert_fusion, f32[32,32]{1,0:T(8,128)S(1)} %broadcast_multiply_fusion, f32[]{:T(128)} %bitcast.7, f32[1,32,32,256]{3,2,1,0:T(8,128)S(1)} %copy-done.1, ...), kind=kLoop, calls=%fused_computation.131 | loop fusion | flops 17039360 | bytes 49468424 | tf_op jit(solution)/shard_map/add | solution.py:118
  243.4 2.8 fusion.113
  246.2 1.7 fusion.132
  247.9 1.7 fusion.131
  249.6 1.3 collective-permute-start.4
  250.9 4.6 %collective-permute-start.5 = (f32[4,32,256]{2,1,0:T(8,128)S(1)}, f32[4,32,256]{2,1,0:T(8,128)S(1)}, u32[]{:S(2)}, u32[]{:S(2)}) collective-permute-start(f32[4,32,256]{2,1,0:T(8,128)S(1)} %get-tuple-element.58), channel_id=1, source_target_pairs={{0,8},{8,16},{16,24},{1,9},{9,17},{17,25},{2,10},{10,18},{18,26},{... | collective-permute-start | bytes 393224 | tf_op jit(solution)/shard_map/ppermute | solution.py:15
  255.4 1.7 fusion.130
  257.2 1.0 collective-permute-done.5
  258.3 5.5 %collective-permute-start.6 = (f32[40,4,256]{2,1,0:T(4,128)S(1)}, f32[40,4,256]{2,1,0:T(4,128)S(1)}, u32[]{:S(2)}, u32[]{:S(2)}) collective-permute-start(f32[40,4,256]{2,1,0:T(4,128)S(1)} %get-tuple-element.24), channel_id=1, source_target_pairs={{1,0},{2,1},{3,2},{4,3},{5,4},{6,5},{7,6},{9,8},{10,9},{11,10},{12... | collective-permute-start | bytes 491528 | tf_op jit(solution)/shard_map/ppermute | solution.py:18
  263.9 2.1 collective-permute-start.7
  266.0 1.7 fusion.129
  267.6 5.6 %collective-permute-done.7 = f32[40,4,256]{2,1,0:T(4,128)S(1)} collective-permute-done((f32[40,4,256]{2,1,0:T(4,128)S(1)}, f32[40,4,256]{2,1,0:T(4,128)S(1)}, u32[]{:S(2)}, u32[]{:S(2)}) %collective-permute-start.7) | collective-permute-done | bytes 163872 | tf_op jit(solution)/shard_map/ppermute | solution.py:15
  273.2 2.0 pad_maximum_fusion.1
  275.1 12.0 %fusion.69 = (f32[32,32,256]{2,1,0:T(8,128)S(1)}, f32[32,32,256]{2,1,0:T(8,128)}, f32[32,32,256]{2,1,0:T(8,128)}) fusion(f32[32,32,256]{2,1,0:T(8,128)S(1)} %get-tuple-element.11, f32[]{:T(128)} %bitcast.12, f32[256]{0:T(256)S(1)} %compare_convert_fusion, f32[32,32]{1,0:T(8,128)S(1)} %broadcast_multiply_fusion, f32[1,32,32,256]{3,2,1,0:T(8,128)S(1)} %copy-done.1, ...), kind=kLoop, calls=%fused_computation.132 | loop fusion | flops 17039360 | bytes 48419848 | tf_op jit(solution)/shard_map/add | solution.py:118
  287.2 2.4 multiply_add_fusion.3
  289.6 1.7 fusion.127
  291.3 1.7 fusion.126
  293.0 1.3 collective-permute-start.8
  294.3 5.0 %collective-permute-start.9 = (f32[4,32,256]{2,1,0:T(8,128)S(1)}, f32[4,32,256]{2,1,0:T(8,128)S(1)}, u32[]{:S(2)}, u32[]{:S(2)}) collective-permute-start(f32[4,32,256]{2,1,0:T(8,128)S(1)} %get-tuple-element.48), channel_id=1, source_target_pairs={{0,8},{8,16},{16,24},{1,9},{9,17},{17,25},{2,10},{10,18},{18,26},{... | collective-permute-start | bytes 393224 | tf_op jit(solution)/shard_map/ppermute | solution.py:15
  299.3 1.7 fusion.125
  301.0 0.8 collective-permute-done.9
  301.8 1.9 collective-permute-start.10
  303.7 3.9 %collective-permute-start.11 = (f32[40,4,256]{2,1,0:T(4,128)S(1)}, f32[40,4,256]{2,1,0:T(4,128)S(1)}, u32[]{:S(2)}, u32[]{:S(2)}) collective-permute-start(f32[40,4,256]{2,1,0:T(4,128)S(1)} %get-tuple-element.21), channel_id=1, source_target_pairs={{0,1},{1,2},{2,3},{3,4},{4,5},{5,6},{6,7},{8,9},{9,10},{10,11},{11... | collective-permute-start | bytes 491528 | tf_op jit(solution)/shard_map/ppermute | solution.py:15
  307.7 1.6 fusion.124
  309.3 3.7 collective-permute-done.11
  313.1 2.0 pad_maximum_fusion.2
  315.0 12.0 %fusion.70 = (f32[32,32,256]{2,1,0:T(8,128)S(1)}, f32[32,32,256]{2,1,0:T(8,128)}, f32[32,32,256]{2,1,0:T(8,128)}) fusion(f32[32,32,256]{2,1,0:T(8,128)S(1)} %copy-done.3, f32[32,32,256]{2,1,0:T(8,128)S(1)} %get-tuple-element.8, f32[]{:T(128)} %bitcast.13, f32[256]{0:T(256)S(1)} %compare_convert_fusion, f32[32,32]{1,0:T(8,128)S(1)} %broadcast_multiply_fusion, ...), kind=kLoop, calls=%fused_computation.133 | loop fusion | flops 17039360 | bytes 48419848 | tf_op jit(solution)/shard_map/add | solution.py:118
  327.0 2.4 multiply_add_fusion.1
  329.4 1.7 fusion.122
  331.1 1.7 fusion.121
  332.9 1.3 collective-permute-start.12
  334.2 5.0 %collective-permute-start.13 = (f32[4,32,256]{2,1,0:T(8,128)S(1)}, f32[4,32,256]{2,1,0:T(8,128)S(1)}, u32[]{:S(2)}, u32[]{:S(2)}) collective-permute-start(f32[4,32,256]{2,1,0:T(8,128)S(1)} %get-tuple-element.38), channel_id=1, source_target_pairs={{0,8},{8,16},{16,24},{1,9},{9,17},{17,25},{2,10},{10,18},{18,26},{... | collective-permute-start | bytes 393224 | tf_op jit(solution)/shard_map/ppermute | solution.py:15
  339.1 1.8 fusion.120
  340.9 0.7 collective-permute-done.13
  341.7 1.9 collective-permute-start.14
  343.6 4.1 %collective-permute-start.15 = (f32[40,4,256]{2,1,0:T(4,128)S(1)}, f32[40,4,256]{2,1,0:T(4,128)S(1)}, u32[]{:S(2)}, u32[]{:S(2)}) collective-permute-start(f32[40,4,256]{2,1,0:T(4,128)S(1)} %get-tuple-element.17), channel_id=1, source_target_pairs={{0,1},{1,2},{2,3},{3,4},{4,5},{5,6},{6,7},{8,9},{9,10},{10,11},{11... | collective-permute-start | bytes 491528 | tf_op jit(solution)/shard_map/ppermute | solution.py:15
  347.8 1.7 fusion.119
  349.5 3.5 collective-permute-done.15
  353.0 2.0 pad_maximum_fusion.3
  354.9 10.7 %add_bitcast_fusion = (f32[1,32,32,256]{3,2,1,0:T(8,128)}, f32[32,32,256]{2,1,0:T(8,128)S(1)}, f32[32,32,256]{2,1,0:T(8,128)}) fusion(f32[32,32,256]{2,1,0:T(8,128)S(1)} %multiply_add_fusion.3, f32[32,32,256]{2,1,0:T(8,128)S(1)} %multiply_add_fusion.1, s32[]{:T(128)S(6)} %min.6, bf16[512,32,256]{2,1,0:T(8,128)(2,1)S(1)} %bitcast.36, ...), kind=kLoop, calls=%fused_computation.204 | loop fusion | flops 15204352 | bytes 40026116 | tf_op jit(solution)/shard_map/broadcast_in_dim | solution.py:120
  365.6 4.1 %fusion.72 = f32[1,32,32,256]{3,2,1,0:T(8,128)} fusion(f32[32,32,256]{2,1,0:T(8,128)} %get-tuple-element.4, f32[32,32,256]{2,1,0:T(8,128)S(1)} %get-tuple-element.3, f32[32,32,256]{2,1,0:T(8,128)S(1)} %get-tuple-element.8, f32[32,32,256]{2,1,0:T(8,128)S(1)} %get-tuple-element.5, f32[]{:T(128)} %bitcast.14, f32[256]{0:T(256)S(1)} %compare_convert_fusion, ...), kind=kLoop, calls=%fused_computation.135 | loop fusion | flops 4718592 | bytes 30413832 | tf_op jit(solution)/shard_map/broadcast_in_dim | solution.py:120
  (38 shorter events, 0.4 us)
Async XLA Ops:
  7.2 151.3 %all-gather.3.cloned.1.call-start = ((), (), s32[]{:S(2)}) async-start(), calls=%async_computation.1 | async-start | bytes 8912896 | tf_op jit(solution)/shard_map/all_gather | solution.py:91
  7.9 223.0 %all-gather.5.cloned.1.call-start = ((), (), s32[]{:S(2)}) async-start(), calls=%async_computation.2 | async-start | bytes 8912896 | tf_op jit(solution)/shard_map/all_gather | solution.py:98
  14.0 7.2 %copy-start.1 = (f32[1,32,32,256]{3,2,1,0:T(8,128)S(1)}, f32[1,32,32,256]{3,2,1,0:T(8,128)}, u32[]{:S(2)}) copy-start(f32[1,32,32,256]{3,2,1,0:T(8,128)} %param.16) | copy-start | bytes 3145732
  14.0 13.1 %copy-start.5 = (s32[1,3]{1,0:T(1,128)S(1)}, s32[1,3]{1,0:T(1,128)}, u32[]{:S(2)}) copy-start(s32[1,3]{1,0:T(1,128)} %param.14) | copy-start | bytes 40
  14.0 15.0 %copy-start = (f32[1,32,32,256]{3,2,1,0:T(8,128)S(1)}, f32[1,32,32,256]{3,2,1,0:T(8,128)}, u32[]{:S(2)}) copy-start(f32[1,32,32,256]{3,2,1,0:T(8,128)} %param.18) | copy-start | bytes 3145732
  14.0 139.0 %all-to-all-start = ((bf16[16,32,32,256]{3,2,1,0:T(8,128)(2,1)}), bf16[16,32,32,256]{3,2,1,0:T(8,128)(2,1)}, u32[]{:S(2)}, u32[]{:S(2)}) async-start(bf16[16,32,32,256]{3,2,1,0:T(8,128)(2,1)} %stack.2), calls=%async_computation | async-start | bytes 16777216 | tf_op jit(solution)/shard_map/all_to_all | solution.py:93
  21.2 114.1 %collective-permute-start = (f32[4,32,256]{2,1,0:T(8,128)S(1)}, f32[4,32,256]{2,1,0:T(8,128)S(1)}, u32[]{:S(2)}, u32[]{:S(2)}) collective-permute-start(f32[4,32,256]{2,1,0:T(8,128)S(1)} %get-tuple-element.69), channel_id=1, source_target_pairs={{8,0},{16,8},{24,16},{9,1},{17,9},{25,17},{10,2},{18,10},{26,18},{... | collective-permute-start | bytes 393224 | tf_op jit(solution)/shard_map/ppermute | solution.py:18
  22.5 112.8 %collective-permute-start.1 = (f32[4,32,256]{2,1,0:T(8,128)S(1)}, f32[4,32,256]{2,1,0:T(8,128)S(1)}, u32[]{:S(2)}, u32[]{:S(2)}) collective-permute-start(f32[4,32,256]{2,1,0:T(8,128)S(1)} %get-tuple-element.68), channel_id=1, source_target_pairs={{0,8},{8,16},{16,24},{1,9},{9,17},{17,25},{2,10},{10,18},{18,26},{... | collective-permute-start | bytes 393224 | tf_op jit(solution)/shard_map/ppermute | solution.py:15
  35.8 108.0 %copy-start.6 = (s32[4]{0:T(128)S(1)}, s32[4]{0:T(128)}, u32[]{:S(2)}) copy-start(s32[4]{0:T(128)} %param.13) | copy-start | bytes 52
  35.8 109.2 %copy-start.4 = (f32[1,4]{1,0:T(1,128)S(1)}, f32[1,4]{1,0:T(1,128)}, u32[]{:S(2)}) copy-start(f32[1,4]{1,0:T(1,128)} %param.15) | copy-start | bytes 52
  135.4 10.2 %collective-permute-start.2 = (f32[40,4,256]{2,1,0:T(4,128)S(1)}, f32[40,4,256]{2,1,0:T(4,128)S(1)}, u32[]{:S(2)}, u32[]{:S(2)}) collective-permute-start(f32[40,4,256]{2,1,0:T(4,128)S(1)} %get-tuple-element.28), channel_id=1, source_target_pairs={{1,0},{2,1},{3,2},{4,3},{5,4},{6,5},{7,6},{9,8},{10,9},{11,10},{12... | collective-permute-start | bytes 491528 | tf_op jit(solution)/shard_map/ppermute | solution.py:18
  141.3 9.6 %collective-permute-start.3 = (f32[40,4,256]{2,1,0:T(4,128)S(1)}, f32[40,4,256]{2,1,0:T(4,128)S(1)}, u32[]{:S(2)}, u32[]{:S(2)}) collective-permute-start(f32[40,4,256]{2,1,0:T(4,128)S(1)} %get-tuple-element.29), channel_id=1, source_target_pairs={{0,1},{1,2},{2,3},{3,4},{4,5},{5,6},{6,7},{8,9},{9,10},{10,11},{11... | collective-permute-start | bytes 491528 | tf_op jit(solution)/shard_map/ppermute | solution.py:15
  230.9 12.5 %slice-start = ((s8[8388608]{0:T(1024)(128)(4,1)}), s8[4194304]{0:T(1024)(128)(4,1)S(1)}, s32[]{:S(2)}) async-start(s8[8388608]{0:T(1024)(128)(4,1)} %bitcast.35), calls=%async_computation.3 | async-start | bytes 8388608
  230.9 12.5 %slice-start.1 = ((s8[8388608]{0:T(1024)(128)(4,1)}), s8[4194304]{0:T(1024)(128)(4,1)S(1)}, s32[]{:S(2)}) async-start(s8[8388608]{0:T(1024)(128)(4,1)} %bitcast.35), calls=%async_computation.4 | async-start | bytes 8388608
  243.4 31.8 %copy-start.2 = (f32[32,32,256]{2,1,0:T(8,128)}, f32[32,32,256]{2,1,0:T(8,128)S(1)}, u32[]{:S(2)}) copy-start(f32[32,32,256]{2,1,0:T(8,128)S(1)} %get-tuple-element.11) | copy-start | bytes 3145732
  249.6 7.6 %collective-permute-start.4 = (f32[4,32,256]{2,1,0:T(8,128)S(1)}, f32[4,32,256]{2,1,0:T(8,128)S(1)}, u32[]{:S(2)}, u32[]{:S(2)}) collective-permute-start(f32[4,32,256]{2,1,0:T(8,128)S(1)} %get-tuple-element.59), channel_id=1, source_target_pairs={{8,0},{16,8},{24,16},{9,1},{17,9},{25,17},{10,2},{18,10},{26,18},{... | collective-permute-start | bytes 393224 | tf_op jit(solution)/shard_map/ppermute | solution.py:18
  250.9 7.4 %collective-permute-start.5 = (f32[4,32,256]{2,1,0:T(8,128)S(1)}, f32[4,32,256]{2,1,0:T(8,128)S(1)}, u32[]{:S(2)}, u32[]{:S(2)}) collective-permute-start(f32[4,32,256]{2,1,0:T(8,128)S(1)} %get-tuple-element.58), channel_id=1, source_target_pairs={{0,8},{8,16},{16,24},{1,9},{9,17},{17,25},{2,10},{10,18},{18,26},{... | collective-permute-start | bytes 393224 | tf_op jit(solution)/shard_map/ppermute | solution.py:15
  258.3 9.3 %collective-permute-start.6 = (f32[40,4,256]{2,1,0:T(4,128)S(1)}, f32[40,4,256]{2,1,0:T(4,128)S(1)}, u32[]{:S(2)}, u32[]{:S(2)}) collective-permute-start(f32[40,4,256]{2,1,0:T(4,128)S(1)} %get-tuple-element.24), channel_id=1, source_target_pairs={{1,0},{2,1},{3,2},{4,3},{5,4},{6,5},{7,6},{9,8},{10,9},{11,10},{12... | collective-permute-start | bytes 491528 | tf_op jit(solution)/shard_map/ppermute | solution.py:18
  263.9 9.3 %collective-permute-start.7 = (f32[40,4,256]{2,1,0:T(4,128)S(1)}, f32[40,4,256]{2,1,0:T(4,128)S(1)}, u32[]{:S(2)}, u32[]{:S(2)}) collective-permute-start(f32[40,4,256]{2,1,0:T(4,128)S(1)} %get-tuple-element.25), channel_id=1, source_target_pairs={{0,1},{1,2},{2,3},{3,4},{4,5},{5,6},{6,7},{8,9},{9,10},{10,11},{11... | collective-permute-start | bytes 491528 | tf_op jit(solution)/shard_map/ppermute | solution.py:15
  293.0 8.0 %collective-permute-start.8 = (f32[4,32,256]{2,1,0:T(8,128)S(1)}, f32[4,32,256]{2,1,0:T(8,128)S(1)}, u32[]{:S(2)}, u32[]{:S(2)}) collective-permute-start(f32[4,32,256]{2,1,0:T(8,128)S(1)} %get-tuple-element.49), channel_id=1, source_target_pairs={{8,0},{16,8},{24,16},{9,1},{17,9},{25,17},{10,2},{18,10},{26,18},{... | collective-permute-start | bytes 393224 | tf_op jit(solution)/shard_map/ppermute | solution.py:18
  294.3 7.5 %collective-permute-start.9 = (f32[4,32,256]{2,1,0:T(8,128)S(1)}, f32[4,32,256]{2,1,0:T(8,128)S(1)}, u32[]{:S(2)}, u32[]{:S(2)}) collective-permute-start(f32[4,32,256]{2,1,0:T(8,128)S(1)} %get-tuple-element.48), channel_id=1, source_target_pairs={{0,8},{8,16},{16,24},{1,9},{9,17},{17,25},{2,10},{10,18},{18,26},{... | collective-permute-start | bytes 393224 | tf_op jit(solution)/shard_map/ppermute | solution.py:15
  301.8 7.5 %collective-permute-start.10 = (f32[40,4,256]{2,1,0:T(4,128)S(1)}, f32[40,4,256]{2,1,0:T(4,128)S(1)}, u32[]{:S(2)}, u32[]{:S(2)}) collective-permute-start(f32[40,4,256]{2,1,0:T(4,128)S(1)} %get-tuple-element.20), channel_id=1, source_target_pairs={{1,0},{2,1},{3,2},{4,3},{5,4},{6,5},{7,6},{9,8},{10,9},{11,10},{12... | collective-permute-start | bytes 491528 | tf_op jit(solution)/shard_map/ppermute | solution.py:18
  303.7 9.3 %collective-permute-start.11 = (f32[40,4,256]{2,1,0:T(4,128)S(1)}, f32[40,4,256]{2,1,0:T(4,128)S(1)}, u32[]{:S(2)}, u32[]{:S(2)}) collective-permute-start(f32[40,4,256]{2,1,0:T(4,128)S(1)} %get-tuple-element.21), channel_id=1, source_target_pairs={{0,1},{1,2},{2,3},{3,4},{4,5},{5,6},{6,7},{8,9},{9,10},{10,11},{11... | collective-permute-start | bytes 491528 | tf_op jit(solution)/shard_map/ppermute | solution.py:15
  309.3 5.7 %copy-start.3 = (f32[32,32,256]{2,1,0:T(8,128)S(1)}, f32[32,32,256]{2,1,0:T(8,128)}, u32[]{:S(2)}) copy-start(f32[32,32,256]{2,1,0:T(8,128)} %copy-done.2) | copy-start | bytes 3145732
  332.9 8.0 %collective-permute-start.12 = (f32[4,32,256]{2,1,0:T(8,128)S(1)}, f32[4,32,256]{2,1,0:T(8,128)S(1)}, u32[]{:S(2)}, u32[]{:S(2)}) collective-permute-start(f32[4,32,256]{2,1,0:T(8,128)S(1)} %get-tuple-element.39), channel_id=1, source_target_pairs={{8,0},{16,8},{24,16},{9,1},{17,9},{25,17},{10,2},{18,10},{26,18},{... | collective-permute-start | bytes 393224 | tf_op jit(solution)/shard_map/ppermute | solution.py:18
  334.2 7.5 %collective-permute-start.13 = (f32[4,32,256]{2,1,0:T(8,128)S(1)}, f32[4,32,256]{2,1,0:T(8,128)S(1)}, u32[]{:S(2)}, u32[]{:S(2)}) collective-permute-start(f32[4,32,256]{2,1,0:T(8,128)S(1)} %get-tuple-element.38), channel_id=1, source_target_pairs={{0,8},{8,16},{16,24},{1,9},{9,17},{17,25},{2,10},{10,18},{18,26},{... | collective-permute-start | bytes 393224 | tf_op jit(solution)/shard_map/ppermute | solution.py:15
  341.7 7.8 %collective-permute-start.14 = (f32[40,4,256]{2,1,0:T(4,128)S(1)}, f32[40,4,256]{2,1,0:T(4,128)S(1)}, u32[]{:S(2)}, u32[]{:S(2)}) collective-permute-start(f32[40,4,256]{2,1,0:T(4,128)S(1)} %get-tuple-element.16), channel_id=1, source_target_pairs={{1,0},{2,1},{3,2},{4,3},{5,4},{6,5},{7,6},{9,8},{10,9},{11,10},{12... | collective-permute-start | bytes 491528 | tf_op jit(solution)/shard_map/ppermute | solution.py:18
  343.6 9.3 %collective-permute-start.15 = (f32[40,4,256]{2,1,0:T(4,128)S(1)}, f32[40,4,256]{2,1,0:T(4,128)S(1)}, u32[]{:S(2)}, u32[]{:S(2)}) collective-permute-start(f32[40,4,256]{2,1,0:T(4,128)S(1)} %get-tuple-element.17), channel_id=1, source_target_pairs={{0,1},{1,2},{2,3},{3,4},{4,5},{5,6},{6,7},{8,9},{9,10},{10,11},{11... | collective-permute-start | bytes 491528 | tf_op jit(solution)/shard_map/ppermute | solution.py:15
Sparse Core Ops, SparseCore 0:
  10.5 147.9 all-gather.2
  160.9 69.9 all-gather.4
